TPU v7x, 32 devices: a whole 2x2x4 slice. The times are simulated.
32 devices in a mesh: dom: 16 (over z, y, core), rep: 2 (over x).
Axes of the slice: x: 2, y: 2, z: 4, core: 2. Of those that a mesh axis runs over, the one named last changes fastest.
Arguments:
- features: bfloat16 [4096, 1024], P('dom'), may hold values from -6 to 6
- tiles: bfloat16 [2, 32, 12, 128, 128], P(None, 'dom'), may hold values from 0 to 2, as said below
- columns: int32 [2, 32, 12], P(None, 'dom'), may hold values from 0 to 31, as said below
- counts: int32 [2, 32], P(None, 'dom'), may hold values from 1 to 12, as said below
- degrees: int32 [2, 4096], P(None, 'dom'), may hold values from 16 to 64
- w_self: bfloat16 [1024, 1024], replicated, may hold values from -0.1875 to 0.1875
- w_in: bfloat16 [1024, 1024], replicated, may hold values from -1 to 1
- w_out: bfloat16 [1024, 1024], replicated, may hold values from -1 to 1
Outputs:
- layer_out: bfloat16 [4096, 1024], P('dom')
Inputs may be any that keep to these rules, and one draw needn't show every extreme that they name: Within one block-row the 12 block-columns are distinct; only the first counts slots are read. `counts`: in each relation some block-row has all 12 slots live. `tiles`: edge weights are zero or positive.
All inputs are finite; a program needn't handle non-finite values.
Results may differ from a plain program's by a relative error of at most 0.0038.
Values may be sent and summed in bfloat16 or wider, within the bound.
No kernel may reach another device: no remote copies, remote signals or barrier semaphores. Data moves between devices by JAX's collectives and lax.ppermute only.
A program may use at most 64 MiB of HBM per device.

v0:
```python
import jax
import jax.numpy as jnp
from jax import lax
from jax.sharding import PartitionSpec as P


def from_behind(block, axis, distance):
    devices = range(lax.axis_size(axis))
    route = [((i - distance) % len(devices), i) for i in devices]
    return lax.ppermute(block, axis, route)


def finish(summed, degree_rows, feature_rows, w_self, w_in, w_out):
    scaled = summed / degree_rows[:, :, None].astype(jnp.float32)
    agg_in = scaled[0].astype(jnp.bfloat16)
    agg_out = scaled[1].astype(jnp.bfloat16)
    hidden = jnp.dot(feature_rows, w_self, preferred_element_type=jnp.float32)
    hidden = hidden + jnp.dot(agg_in, w_in, preferred_element_type=jnp.float32)
    hidden = hidden + jnp.dot(agg_out, w_out, preferred_element_type=jnp.float32)
    return jax.nn.relu(hidden).astype(jnp.bfloat16)


def on_device(features, tiles, columns, counts, degrees, w_self, w_in, w_out):
    node_rows, feat_width = features.shape
    tile_size = tiles.shape[3]
    local_blocks = node_rows // tile_size
    cycle_size = lax.axis_size("dom")
    half_cycle = cycle_size // 2
    position = lax.axis_index("dom")
    replica = lax.axis_index("rep")
    slot_ids = jnp.arange(tiles.shape[2], dtype=jnp.int32)
    block_ids = jnp.arange(local_blocks, dtype=jnp.int32)
    live_slots = slot_ids[None, None, :] < counts[:, :, None]

    def absorb(running, feature_panel, source):
        targets = source * local_blocks + block_ids
        matches = (columns[:, :, None, :] == targets[None, None, :, None]) & live_slots[
            :, :, None, :
        ]
        present = jnp.any(matches, axis=-1)
        picks = jnp.sum(jnp.where(matches, slot_ids, 0), axis=-1)
        chosen = jnp.take_along_axis(tiles, picks[:, :, :, None, None], axis=2)
        chosen = jnp.where(present[:, :, :, None, None], chosen, jnp.zeros_like(chosen))
        panel_blocks = feature_panel.reshape(local_blocks, tile_size, feat_width)
        return running + jnp.einsum(
            "ricab,cbh->riah", chosen, panel_blocks, preferred_element_type=jnp.float32
        )

    running = jnp.zeros((2, local_blocks, tile_size, feat_width), jnp.float32)
    distant = from_behind(features, "dom", half_cycle)
    feature_panel = jnp.where(replica == 0, features, distant)
    anchor = (position - replica * half_cycle) % cycle_size

    def advance(turn, carry):
        sums_now, panel_now = carry
        sums_now = absorb(sums_now, panel_now, (anchor - turn) % cycle_size)
        panel_now = from_behind(panel_now, "dom", 1)
        return (sums_now, panel_now)

    running, feature_panel = lax.fori_loop(0, half_cycle - 1, advance, (running, feature_panel))
    running = absorb(running, feature_panel, (anchor - (half_cycle - 1)) % cycle_size)
    stacked = running.reshape(2, node_rows, feat_width)
    summed = lax.psum(stacked, "rep")
    return finish(summed, degrees, features, w_self, w_in, w_out)


def solution(mesh):
    placed = (
        P("dom", None),
        P(None, "dom", None, None, None),
        P(None, "dom", None),
        P(None, "dom"),
        P(None, "dom"),
        P(),
        P(),
        P(),
    )
    return jax.shard_map(
        on_device, mesh=mesh, in_specs=placed, out_specs=P("dom", None), check_vma=False
    )
```

profile of v0, /device:TPU:0, one launch (start us, length us, event | category | flops | bytes accessed | tf_op | source)
XLA Modules:
  0.0 189.8 jit_solution(7590709612621748421)
XLA Ops:
  6.5 4.1 %collective-permute-start.1 = (bf16[256,1024]{1,0:T(8,128)(2,1)}, bf16[256,1024]{1,0:T(8,128)(2,1)S(1)}, u32[]{:S(2)}, u32[]{:S(2)}) collective-permute-start(bf16[256,1024]{1,0:T(8,128)(2,1)} %param.12), channel_id=1, source_target_pairs={{16,0},{18,2},{20,4},{22,6},{24,8},{26,10},{28,12},{30,14},{0,16},... | collective-permute-start | bytes 1572872 | tf_op jit(solution)/shard_map/ppermute | solution.py:10
  12.4 2.7 %gather_fusion.1 = bf16[8,128,128]{2,1,0:T(8,128)(2,1)} fusion(bf16[2,2,12,128,128]{4,3,2,1,0:T(8,128)(2,1)} %param.13, s32[8]{0:T(128)S(1)} %reshape.89), kind=kCustom, calls=%fused_computation.1.clone | custom fusion | bytes 524384 | tf_op jit(solution)/shard_map/jit(take_along_axis)/gather | solution.py:42
  16.0 18.0 %collective-permute-done.1 = bf16[256,1024]{1,0:T(8,128)(2,1)S(1)} collective-permute-done((bf16[256,1024]{1,0:T(8,128)(2,1)}, bf16[256,1024]{1,0:T(8,128)(2,1)S(1)}, u32[]{:S(2)}, u32[]{:S(2)}) %collective-permute-start.1) | collective-permute-done | bytes 524320 | tf_op jit(solution)/shard_map/ppermute | solution.py:10
  35.1 79.8 %while.18 = (s32[]{:T(128)}, f32[2,2,128,1024]{3,2,1,0:T(8,128)}, bf16[256,1024]{1,0:T(8,128)(2,1)S(1)}, s32[2,2,12]{2,1,0:T(2,128)S(1)}, s32[]{:T(128)}, /*inde...) while((s32[]{:T(128)}, f32[2,2,128,1024]{3,2,1,0:T(8,128)}, ...), condition=%wide.region_3.5_spmd.clone, body=%wide.region_0.4_spmd.clone.sunk | while | flops 269747040 | bytes 8651944 | solution.py:60
  35.9 2.0 %gather_fusion = bf16[8,128,128]{2,1,0:T(8,128)(2,1)S(1)} fusion(bf16[2,2,12,128,128]{4,3,2,1,0:T(8,128)(2,1)} %get-tuple-element.347, s32[8]{0:T(128)S(1)} %reshape.102), kind=kCustom, calls=%fused_computation.clone.clone.1 | custom fusion | bytes 524384 | tf_op jit(solution)/shard_map/while/body/eval_jaxpr/jit(take_along_axis)/gather | solution.py:42
  39.8 6.8 %collective-permute-done = bf16[256,1024]{1,0:T(8,128)(2,1)S(1)} collective-permute-done((bf16[256,1024]{1,0:T(8,128)(2,1)S(1)}, bf16[256,1024]{1,0:T(8,128)(2,1)S(1)}, u32[]{:S(2)}, u32[]{:S(2)}) %collective-permute-start) | collective-permute-done | bytes 524320 | tf_op jit(solution)/shard_map/while/body/eval_jaxpr/ppermute | solution.py:10
  47.3 2.0 %gather_fusion = bf16[8,128,128]{2,1,0:T(8,128)(2,1)S(1)} fusion(bf16[2,2,12,128,128]{4,3,2,1,0:T(8,128)(2,1)} %get-tuple-element.347, s32[8]{0:T(128)S(1)} %reshape.102), kind=kCustom, calls=%fused_computation.clone.clone.1 | custom fusion | bytes 524384 | tf_op jit(solution)/shard_map/while/body/eval_jaxpr/jit(take_along_axis)/gather | solution.py:42
  49.3 3.4 %bitcast_add_fusion.3 = f32[2,2,128,1024]{3,2,1,0:T(8,128)} fusion(f32[2,2,128,1024]{3,2,1,0:T(8,128)} %get-tuple-element.331, bf16[2,128,1024,1,1]{2,1,0,4,3:T(8,128)(2,1)S(1)} %bitcast.71, pred[]{:T(512)S(6)} %compare.6, bf16[2,2,2,128,128]{4,3,2,1,0:T(8,128)(2,1)S(1)} %bitcast.72, pred[2,2,2]{2,1,0:T(4,128)(4,1)S(1)} %and_bitcast_fusion.3, ...), kind=kOutput, calls=%fused_computation.5.clone.1 | convolution fusion | flops 269746176 | bytes 4980753 | tf_op jit(solution)/shard_map/while/body/eval_jaxpr/ricab,cbh->riah/dot_general | solution.py:45
  52.8 5.2 %collective-permute-done = bf16[256,1024]{1,0:T(8,128)(2,1)S(1)} collective-permute-done((bf16[256,1024]{1,0:T(8,128)(2,1)S(1)}, bf16[256,1024]{1,0:T(8,128)(2,1)S(1)}, u32[]{:S(2)}, u32[]{:S(2)}) %collective-permute-start) | collective-permute-done | bytes 524320 | tf_op jit(solution)/shard_map/while/body/eval_jaxpr/ppermute | solution.py:10
  58.7 2.0 %gather_fusion = bf16[8,128,128]{2,1,0:T(8,128)(2,1)S(1)} fusion(bf16[2,2,12,128,128]{4,3,2,1,0:T(8,128)(2,1)} %get-tuple-element.347, s32[8]{0:T(128)S(1)} %reshape.102), kind=kCustom, calls=%fused_computation.clone.clone.1 | custom fusion | bytes 524384 | tf_op jit(solution)/shard_map/while/body/eval_jaxpr/jit(take_along_axis)/gather | solution.py:42
  60.7 3.4 %bitcast_add_fusion.3 = f32[2,2,128,1024]{3,2,1,0:T(8,128)} fusion(f32[2,2,128,1024]{3,2,1,0:T(8,128)} %get-tuple-element.331, bf16[2,128,1024,1,1]{2,1,0,4,3:T(8,128)(2,1)S(1)} %bitcast.71, pred[]{:T(512)S(6)} %compare.6, bf16[2,2,2,128,128]{4,3,2,1,0:T(8,128)(2,1)S(1)} %bitcast.72, pred[2,2,2]{2,1,0:T(4,128)(4,1)S(1)} %and_bitcast_fusion.3, ...), kind=kOutput, calls=%fused_computation.5.clone.1 | convolution fusion | flops 269746176 | bytes 4980753 | tf_op jit(solution)/shard_map/while/body/eval_jaxpr/ricab,cbh->riah/dot_general | solution.py:45
  64.2 5.2 %collective-permute-done = bf16[256,1024]{1,0:T(8,128)(2,1)S(1)} collective-permute-done((bf16[256,1024]{1,0:T(8,128)(2,1)S(1)}, bf16[256,1024]{1,0:T(8,128)(2,1)S(1)}, u32[]{:S(2)}, u32[]{:S(2)}) %collective-permute-start) | collective-permute-done | bytes 524320 | tf_op jit(solution)/shard_map/while/body/eval_jaxpr/ppermute | solution.py:10
  70.1 2.0 %gather_fusion = bf16[8,128,128]{2,1,0:T(8,128)(2,1)S(1)} fusion(bf16[2,2,12,128,128]{4,3,2,1,0:T(8,128)(2,1)} %get-tuple-element.347, s32[8]{0:T(128)S(1)} %reshape.102), kind=kCustom, calls=%fused_computation.clone.clone.1 | custom fusion | bytes 524384 | tf_op jit(solution)/shard_map/while/body/eval_jaxpr/jit(take_along_axis)/gather | solution.py:42
  72.1 3.4 %bitcast_add_fusion.3 = f32[2,2,128,1024]{3,2,1,0:T(8,128)} fusion(f32[2,2,128,1024]{3,2,1,0:T(8,128)} %get-tuple-element.331, bf16[2,128,1024,1,1]{2,1,0,4,3:T(8,128)(2,1)S(1)} %bitcast.71, pred[]{:T(512)S(6)} %compare.6, bf16[2,2,2,128,128]{4,3,2,1,0:T(8,128)(2,1)S(1)} %bitcast.72, pred[2,2,2]{2,1,0:T(4,128)(4,1)S(1)} %and_bitcast_fusion.3, ...), kind=kOutput, calls=%fused_computation.5.clone.1 | convolution fusion | flops 269746176 | bytes 4980753 | tf_op jit(solution)/shard_map/while/body/eval_jaxpr/ricab,cbh->riah/dot_general | solution.py:45
  75.6 5.2 %collective-permute-done = bf16[256,1024]{1,0:T(8,128)(2,1)S(1)} collective-permute-done((bf16[256,1024]{1,0:T(8,128)(2,1)S(1)}, bf16[256,1024]{1,0:T(8,128)(2,1)S(1)}, u32[]{:S(2)}, u32[]{:S(2)}) %collective-permute-start) | collective-permute-done | bytes 524320 | tf_op jit(solution)/shard_map/while/body/eval_jaxpr/ppermute | solution.py:10
  81.5 2.0 %gather_fusion = bf16[8,128,128]{2,1,0:T(8,128)(2,1)S(1)} fusion(bf16[2,2,12,128,128]{4,3,2,1,0:T(8,128)(2,1)} %get-tuple-element.347, s32[8]{0:T(128)S(1)} %reshape.102), kind=kCustom, calls=%fused_computation.clone.clone.1 | custom fusion | bytes 524384 | tf_op jit(solution)/shard_map/while/body/eval_jaxpr/jit(take_along_axis)/gather | solution.py:42
  83.5 3.4 %bitcast_add_fusion.3 = f32[2,2,128,1024]{3,2,1,0:T(8,128)} fusion(f32[2,2,128,1024]{3,2,1,0:T(8,128)} %get-tuple-element.331, bf16[2,128,1024,1,1]{2,1,0,4,3:T(8,128)(2,1)S(1)} %bitcast.71, pred[]{:T(512)S(6)} %compare.6, bf16[2,2,2,128,128]{4,3,2,1,0:T(8,128)(2,1)S(1)} %bitcast.72, pred[2,2,2]{2,1,0:T(4,128)(4,1)S(1)} %and_bitcast_fusion.3, ...), kind=kOutput, calls=%fused_computation.5.clone.1 | convolution fusion | flops 269746176 | bytes 4980753 | tf_op jit(solution)/shard_map/while/body/eval_jaxpr/ricab,cbh->riah/dot_general | solution.py:45
  87.0 5.2 %collective-permute-done = bf16[256,1024]{1,0:T(8,128)(2,1)S(1)} collective-permute-done((bf16[256,1024]{1,0:T(8,128)(2,1)S(1)}, bf16[256,1024]{1,0:T(8,128)(2,1)S(1)}, u32[]{:S(2)}, u32[]{:S(2)}) %collective-permute-start) | collective-permute-done | bytes 524320 | tf_op jit(solution)/shard_map/while/body/eval_jaxpr/ppermute | solution.py:10
  94.9 3.4 %bitcast_add_fusion.3 = f32[2,2,128,1024]{3,2,1,0:T(8,128)} fusion(f32[2,2,128,1024]{3,2,1,0:T(8,128)} %get-tuple-element.331, bf16[2,128,1024,1,1]{2,1,0,4,3:T(8,128)(2,1)S(1)} %bitcast.71, pred[]{:T(512)S(6)} %compare.6, bf16[2,2,2,128,128]{4,3,2,1,0:T(8,128)(2,1)S(1)} %bitcast.72, pred[2,2,2]{2,1,0:T(4,128)(4,1)S(1)} %and_bitcast_fusion.3, ...), kind=kOutput, calls=%fused_computation.5.clone.1 | convolution fusion | flops 269746176 | bytes 4980753 | tf_op jit(solution)/shard_map/while/body/eval_jaxpr/ricab,cbh->riah/dot_general | solution.py:45
  98.4 5.2 %collective-permute-done = bf16[256,1024]{1,0:T(8,128)(2,1)S(1)} collective-permute-done((bf16[256,1024]{1,0:T(8,128)(2,1)S(1)}, bf16[256,1024]{1,0:T(8,128)(2,1)S(1)}, u32[]{:S(2)}, u32[]{:S(2)}) %collective-permute-start) | collective-permute-done | bytes 524320 | tf_op jit(solution)/shard_map/while/body/eval_jaxpr/ppermute | solution.py:10
  104.3 2.0 %gather_fusion = bf16[8,128,128]{2,1,0:T(8,128)(2,1)S(1)} fusion(bf16[2,2,12,128,128]{4,3,2,1,0:T(8,128)(2,1)} %get-tuple-element.347, s32[8]{0:T(128)S(1)} %reshape.102), kind=kCustom, calls=%fused_computation.clone.clone.1 | custom fusion | bytes 524384 | tf_op jit(solution)/shard_map/while/body/eval_jaxpr/jit(take_along_axis)/gather | solution.py:42
  106.3 3.4 %bitcast_add_fusion.3 = f32[2,2,128,1024]{3,2,1,0:T(8,128)} fusion(f32[2,2,128,1024]{3,2,1,0:T(8,128)} %get-tuple-element.331, bf16[2,128,1024,1,1]{2,1,0,4,3:T(8,128)(2,1)S(1)} %bitcast.71, pred[]{:T(512)S(6)} %compare.6, bf16[2,2,2,128,128]{4,3,2,1,0:T(8,128)(2,1)S(1)} %bitcast.72, pred[2,2,2]{2,1,0:T(4,128)(4,1)S(1)} %and_bitcast_fusion.3, ...), kind=kOutput, calls=%fused_computation.5.clone.1 | convolution fusion | flops 269746176 | bytes 4980753 | tf_op jit(solution)/shard_map/while/body/eval_jaxpr/ricab,cbh->riah/dot_general | solution.py:45
  109.7 5.2 %collective-permute-done = bf16[256,1024]{1,0:T(8,128)(2,1)S(1)} collective-permute-done((bf16[256,1024]{1,0:T(8,128)(2,1)S(1)}, bf16[256,1024]{1,0:T(8,128)(2,1)S(1)}, u32[]{:S(2)}, u32[]{:S(2)}) %collective-permute-start) | collective-permute-done | bytes 524320 | tf_op jit(solution)/shard_map/while/body/eval_jaxpr/ppermute | solution.py:10
  120.8 56.9 %all-reduce.2.cloned.1.call-done = f32[2,256,1024]{2,1,0:T(8,128)} async-done(((f32[2,256,1024]{2,1,0:T(8,128)}), f32[2,256,1024]{2,1,0:T(8,128)}) %all-reduce.2.cloned.1.call-update) | async-done | bytes 2097168 | tf_op jit(solution)/shard_map/psum | solution.py:63
  (97 shorter events, 23.7 us)
Async XLA Ops:
  6.5 112.4 %copy-start = (bf16[1024,1024]{1,0:T(8,128)(2,1)S(1)}, bf16[1024,1024]{1,0:T(8,128)(2,1)}, u32[]{:S(2)}) copy-start(bf16[1024,1024]{1,0:T(8,128)(2,1)} %param.17) | copy-start | bytes 6291460
  6.5 28.6 %copy-start.5 = (s32[2,2]{1,0:T(2,128)S(1)}, s32[2,2]{1,0:T(2,128)}, u32[]{:S(2)}) copy-start(s32[2,2]{1,0:T(2,128)} %param.15) | copy-start | bytes 52
  6.5 28.6 %copy-start.4 = (s32[2,2,12]{2,1,0:T(2,128)S(1)}, s32[2,2,12]{2,1,0:T(2,128)}, u32[]{:S(2)}) copy-start(s32[2,2,12]{2,1,0:T(2,128)} %param.14) | copy-start | bytes 580
  6.5 171.1 %all-reduce.2.cloned.1.call-start = ((), (), s32[]{:S(2)}) async-start(), calls=%async_computation | async-start | bytes 4194304 | tf_op jit(solution)/shard_map/psum | solution.py:63
  6.5 27.5 %collective-permute-start.1 = (bf16[256,1024]{1,0:T(8,128)(2,1)}, bf16[256,1024]{1,0:T(8,128)(2,1)S(1)}, u32[]{:S(2)}, u32[]{:S(2)}) collective-permute-start(bf16[256,1024]{1,0:T(8,128)(2,1)} %param.12), channel_id=1, source_target_pairs={{16,0},{18,2},{20,4},{22,6},{24,8},{26,10},{28,12},{30,14},{0,16},... | collective-permute-start | bytes 1572872 | tf_op jit(solution)/shard_map/ppermute | solution.py:10
  35.2 11.4 %collective-permute-start = (bf16[256,1024]{1,0:T(8,128)(2,1)S(1)}, bf16[256,1024]{1,0:T(8,128)(2,1)S(1)}, u32[]{:S(2)}, u32[]{:S(2)}) collective-permute-start(bf16[256,1024]{1,0:T(8,128)(2,1)S(1)} %copy.18), channel_id=1, source_target_pairs={{30,0},{0,2},{2,4},{4,6},{6,8},{8,10},{10,12},{12,14},{14,16},{16,... | collective-permute-start | bytes 1572872 | tf_op jit(solution)/shard_map/while/body/eval_jaxpr/ppermute | solution.py:10
  46.6 11.4 %collective-permute-start = (bf16[256,1024]{1,0:T(8,128)(2,1)S(1)}, bf16[256,1024]{1,0:T(8,128)(2,1)S(1)}, u32[]{:S(2)}, u32[]{:S(2)}) collective-permute-start(bf16[256,1024]{1,0:T(8,128)(2,1)S(1)} %copy.18), channel_id=1, source_target_pairs={{30,0},{0,2},{2,4},{4,6},{6,8},{8,10},{10,12},{12,14},{14,16},{16,... | collective-permute-start | bytes 1572872 | tf_op jit(solution)/shard_map/while/body/eval_jaxpr/ppermute | solution.py:10
  58.0 11.4 %collective-permute-start = (bf16[256,1024]{1,0:T(8,128)(2,1)S(1)}, bf16[256,1024]{1,0:T(8,128)(2,1)S(1)}, u32[]{:S(2)}, u32[]{:S(2)}) collective-permute-start(bf16[256,1024]{1,0:T(8,128)(2,1)S(1)} %copy.18), channel_id=1, source_target_pairs={{30,0},{0,2},{2,4},{4,6},{6,8},{8,10},{10,12},{12,14},{14,16},{16,... | collective-permute-start | bytes 1572872 | tf_op jit(solution)/shard_map/while/body/eval_jaxpr/ppermute | solution.py:10
  69.4 11.4 %collective-permute-start = (bf16[256,1024]{1,0:T(8,128)(2,1)S(1)}, bf16[256,1024]{1,0:T(8,128)(2,1)S(1)}, u32[]{:S(2)}, u32[]{:S(2)}) collective-permute-start(bf16[256,1024]{1,0:T(8,128)(2,1)S(1)} %copy.18), channel_id=1, source_target_pairs={{30,0},{0,2},{2,4},{4,6},{6,8},{8,10},{10,12},{12,14},{14,16},{16,... | collective-permute-start | bytes 1572872 | tf_op jit(solution)/shard_map/while/body/eval_jaxpr/ppermute | solution.py:10
  80.8 11.4 %collective-permute-start = (bf16[256,1024]{1,0:T(8,128)(2,1)S(1)}, bf16[256,1024]{1,0:T(8,128)(2,1)S(1)}, u32[]{:S(2)}, u32[]{:S(2)}) collective-permute-start(bf16[256,1024]{1,0:T(8,128)(2,1)S(1)} %copy.18), channel_id=1, source_target_pairs={{30,0},{0,2},{2,4},{4,6},{6,8},{8,10},{10,12},{12,14},{14,16},{16,... | collective-permute-start | bytes 1572872 | tf_op jit(solution)/shard_map/while/body/eval_jaxpr/ppermute | solution.py:10
  92.2 11.4 %collective-permute-start = (bf16[256,1024]{1,0:T(8,128)(2,1)S(1)}, bf16[256,1024]{1,0:T(8,128)(2,1)S(1)}, u32[]{:S(2)}, u32[]{:S(2)}) collective-permute-start(bf16[256,1024]{1,0:T(8,128)(2,1)S(1)} %copy.18), channel_id=1, source_target_pairs={{30,0},{0,2},{2,4},{4,6},{6,8},{8,10},{10,12},{12,14},{14,16},{16,... | collective-permute-start | bytes 1572872 | tf_op jit(solution)/shard_map/while/body/eval_jaxpr/ppermute | solution.py:10
  103.6 11.4 %collective-permute-start = (bf16[256,1024]{1,0:T(8,128)(2,1)S(1)}, bf16[256,1024]{1,0:T(8,128)(2,1)S(1)}, u32[]{:S(2)}, u32[]{:S(2)}) collective-permute-start(bf16[256,1024]{1,0:T(8,128)(2,1)S(1)} %copy.18), channel_id=1, source_target_pairs={{30,0},{0,2},{2,4},{4,6},{6,8},{8,10},{10,12},{12,14},{14,16},{16,... | collective-permute-start | bytes 1572872 | tf_op jit(solution)/shard_map/while/body/eval_jaxpr/ppermute | solution.py:10
  114.9 1.7 copy-start.1
  118.3 0.7 copy-start.6
  177.6 2.2 %copy-start.2 = (bf16[1024,1024]{1,0:T(8,128)(2,1)S(1)}, bf16[1024,1024]{1,0:T(8,128)(2,1)}, u32[]{:S(2)}) copy-start(bf16[1024,1024]{1,0:T(8,128)(2,1)} %param.18) | copy-start | bytes 6291460
  179.9 1.6 copy-start.3
Sparse Core Ops, SparseCore 0:
  118.4 59.1 all-reduce.1
where the time goes:
time: 191 us; the launch traced here: 190 us
  waiting for transfers between devices  113 us (59%)
  matrix products  28.1 us (15%)
  local copies, waits for them, and re-layouts  19.5 us (10%)
  between operations  13.5 us (7%)
  other arithmetic  11.1 us (6%)
  starting transfers between devices  4.51 us (2%)
    psum x1, waiting for transfers between devices, on_device(): summed = lax.psum(stacked, 'rep')  56.9 us
    ppermute x8, waiting for transfers between devices, from_behind(): return lax.ppermute(block, axis, route)  55.8 us
    dot_general x8, matrix products, absorb(): jnp.einsum('ricab,cbh->riah', chosen, panel_blocks, preferred_element_typ...  24 us
    gather x16, local copies, waits for them, and re-layouts, absorb(): chosen = jnp.take_along_axis(tiles, picks[:, :, :, None, None], axis=2)  17.5 us
    ppermute x8, starting transfers between devices, from_behind(): return lax.ppermute(block, axis, route)  4.51 us
  transfers between devices with their start and end apart: 9, of which 9 were waited for; matrix products, arithmetic and copies ran while one was open for 25% of the time, Pallas kernels for 0%

commit v1 on v0

--- a/solution.py
+++ b/solution.py
@@ -60,7 +60,7 @@
     running, feature_panel = lax.fori_loop(0, half_cycle - 1, advance, (running, feature_panel))
     running = absorb(running, feature_panel, (anchor - (half_cycle - 1)) % cycle_size)
     stacked = running.reshape(2, node_rows, feat_width)
-    summed = lax.psum(stacked, "rep")
+    summed = jnp.sum(lax.all_gather(stacked, "rep"), axis=0)
     return finish(summed, degrees, features, w_self, w_in, w_out)
 
 

time: 191 us -> 189 us (0.990)
  waiting for transfers between devices: 113 us -> 107 us
  other arithmetic: 11.1 us -> 15.2 us
    psum x1 -> x0, waiting for transfers between devices: 56.9 us -> none  [on_device(): summed = lax.psum(stacked, 'rep')]
    all_gather x0 -> x1, waiting for transfers between devices: none -> 50.8 us  [on_device(): summed = jnp.sum(lax.all_gather(stacked, 'rep'), axis=0)]
    reduce_sum x0 -> x1, other arithmetic: none -> 4.12 us  [on_device(): summed = jnp.sum(lax.all_gather(stacked, 'rep'), axis=0)]
  transfers between devices with their start and end apart: 9 -> 9, of which waited for: 9 -> 9; matrix products, arithmetic and copies ran while one was open for 25% -> 26% of each run, Pallas kernels for 0% -> 0%
where the time goes in v1:
time: 189 us; the launch traced here: 188 us
  waiting for transfers between devices  107 us (57%)
  matrix products  28 us (15%)
  local copies, waits for them, and re-layouts  19.5 us (10%)
  other arithmetic  15.2 us (8%)
  between operations  13.5 us (7%)
  starting transfers between devices  4.51 us (2%)
    ppermute x8, waiting for transfers between devices, from_behind(): return lax.ppermute(block, axis, route)  55.8 us
    all_gather x1, waiting for transfers between devices, on_device(): summed = jnp.sum(lax.all_gather(stacked, 'rep'), axis=0)  50.8 us
    dot_general x8, matrix products, absorb(): jnp.einsum('ricab,cbh->riah', chosen, panel_blocks, preferred_element_typ...  24 us
    gather x16, local copies, waits for them, and re-layouts, absorb(): chosen = jnp.take_along_axis(tiles, picks[:, :, :, None, None], axis=2)  17.5 us
    ppermute x8, starting transfers between devices, from_behind(): return lax.ppermute(block, axis, route)  4.51 us
    reduce_sum x1, other arithmetic, on_device(): summed = jnp.sum(lax.all_gather(stacked, 'rep'), axis=0)  4.12 us
  transfers between devices with their start and end apart: 9, of which 9 were waited for; matrix products, arithmetic and copies ran while one was open for 26% of the time, Pallas kernels for 0%

profile of v1, /device:TPU:0, one launch (start us, length us, event | category | flops | bytes accessed | tf_op | source)
XLA Modules:
  0.0 187.8 jit_solution(18121934693025499640)
XLA Ops:
  6.5 4.1 %collective-permute-start.1 = (bf16[256,1024]{1,0:T(8,128)(2,1)}, bf16[256,1024]{1,0:T(8,128)(2,1)S(1)}, u32[]{:S(2)}, u32[]{:S(2)}) collective-permute-start(bf16[256,1024]{1,0:T(8,128)(2,1)} %param.12), channel_id=1, source_target_pairs={{16,0},{18,2},{20,4},{22,6},{24,8},{26,10},{28,12},{30,14},{0,16},... | collective-permute-start | bytes 1572872 | tf_op jit(solution)/shard_map/ppermute | solution.py:10
  12.4 2.7 %gather_fusion.1 = bf16[8,128,128]{2,1,0:T(8,128)(2,1)} fusion(bf16[2,2,12,128,128]{4,3,2,1,0:T(8,128)(2,1)} %param.13, s32[8]{0:T(128)S(1)} %reshape.85), kind=kCustom, calls=%fused_computation.1.clone | custom fusion | bytes 524384 | tf_op jit(solution)/shard_map/jit(take_along_axis)/gather | solution.py:42
  16.0 18.0 %collective-permute-done.1 = bf16[256,1024]{1,0:T(8,128)(2,1)S(1)} collective-permute-done((bf16[256,1024]{1,0:T(8,128)(2,1)}, bf16[256,1024]{1,0:T(8,128)(2,1)S(1)}, u32[]{:S(2)}, u32[]{:S(2)}) %collective-permute-start.1) | collective-permute-done | bytes 524320 | tf_op jit(solution)/shard_map/ppermute | solution.py:10
  35.1 79.8 %while.18 = (s32[]{:T(128)}, f32[2,2,128,1024]{3,2,1,0:T(8,128)}, bf16[256,1024]{1,0:T(8,128)(2,1)S(1)}, s32[2,2,12]{2,1,0:T(2,128)S(1)}, s32[]{:T(128)}, /*inde...) while((s32[]{:T(128)}, f32[2,2,128,1024]{3,2,1,0:T(8,128)}, ...), condition=%wide.region_3.5_spmd.clone, body=%wide.region_0.4_spmd.clone.sunk | while | flops 269747040 | bytes 8651944 | solution.py:60
  35.9 2.0 %gather_fusion = bf16[8,128,128]{2,1,0:T(8,128)(2,1)S(1)} fusion(bf16[2,2,12,128,128]{4,3,2,1,0:T(8,128)(2,1)} %get-tuple-element.347, s32[8]{0:T(128)S(1)} %reshape.98), kind=kCustom, calls=%fused_computation.clone.clone.1 | custom fusion | bytes 524384 | tf_op jit(solution)/shard_map/while/body/eval_jaxpr/jit(take_along_axis)/gather | solution.py:42
  39.8 6.8 %collective-permute-done = bf16[256,1024]{1,0:T(8,128)(2,1)S(1)} collective-permute-done((bf16[256,1024]{1,0:T(8,128)(2,1)S(1)}, bf16[256,1024]{1,0:T(8,128)(2,1)S(1)}, u32[]{:S(2)}, u32[]{:S(2)}) %collective-permute-start) | collective-permute-done | bytes 524320 | tf_op jit(solution)/shard_map/while/body/eval_jaxpr/ppermute | solution.py:10
  49.3 3.4 %bitcast_add_fusion.3 = f32[2,2,128,1024]{3,2,1,0:T(8,128)} fusion(f32[2,2,128,1024]{3,2,1,0:T(8,128)} %get-tuple-element.331, bf16[2,128,1024,1,1]{2,1,0,4,3:T(8,128)(2,1)S(1)} %bitcast.71, pred[]{:T(512)S(6)} %compare.6, bf16[2,2,2,128,128]{4,3,2,1,0:T(8,128)(2,1)S(1)} %bitcast.72, pred[2,2,2]{2,1,0:T(4,128)(4,1)S(1)} %and_bitcast_fusion.3, ...), kind=kOutput, calls=%fused_computation.5.clone.1 | convolution fusion | flops 269746176 | bytes 4980753 | tf_op jit(solution)/shard_map/while/body/eval_jaxpr/ricab,cbh->riah/dot_general | solution.py:45
  52.8 5.2 %collective-permute-done = bf16[256,1024]{1,0:T(8,128)(2,1)S(1)} collective-permute-done((bf16[256,1024]{1,0:T(8,128)(2,1)S(1)}, bf16[256,1024]{1,0:T(8,128)(2,1)S(1)}, u32[]{:S(2)}, u32[]{:S(2)}) %collective-permute-start) | collective-permute-done | bytes 524320 | tf_op jit(solution)/shard_map/while/body/eval_jaxpr/ppermute | solution.py:10
  58.7 2.0 %gather_fusion = bf16[8,128,128]{2,1,0:T(8,128)(2,1)S(1)} fusion(bf16[2,2,12,128,128]{4,3,2,1,0:T(8,128)(2,1)} %get-tuple-element.347, s32[8]{0:T(128)S(1)} %reshape.98), kind=kCustom, calls=%fused_computation.clone.clone.1 | custom fusion | bytes 524384 | tf_op jit(solution)/shard_map/while/body/eval_jaxpr/jit(take_along_axis)/gather | solution.py:42
  60.7 3.4 %bitcast_add_fusion.3 = f32[2,2,128,1024]{3,2,1,0:T(8,128)} fusion(f32[2,2,128,1024]{3,2,1,0:T(8,128)} %get-tuple-element.331, bf16[2,128,1024,1,1]{2,1,0,4,3:T(8,128)(2,1)S(1)} %bitcast.71, pred[]{:T(512)S(6)} %compare.6, bf16[2,2,2,128,128]{4,3,2,1,0:T(8,128)(2,1)S(1)} %bitcast.72, pred[2,2,2]{2,1,0:T(4,128)(4,1)S(1)} %and_bitcast_fusion.3, ...), kind=kOutput, calls=%fused_computation.5.clone.1 | convolution fusion | flops 269746176 | bytes 4980753 | tf_op jit(solution)/shard_map/while/body/eval_jaxpr/ricab,cbh->riah/dot_general | solution.py:45
  64.2 5.2 %collective-permute-done = bf16[256,1024]{1,0:T(8,128)(2,1)S(1)} collective-permute-done((bf16[256,1024]{1,0:T(8,128)(2,1)S(1)}, bf16[256,1024]{1,0:T(8,128)(2,1)S(1)}, u32[]{:S(2)}, u32[]{:S(2)}) %collective-permute-start) | collective-permute-done | bytes 524320 | tf_op jit(solution)/shard_map/while/body/eval_jaxpr/ppermute | solution.py:10
  72.1 3.4 %bitcast_add_fusion.3 = f32[2,2,128,1024]{3,2,1,0:T(8,128)} fusion(f32[2,2,128,1024]{3,2,1,0:T(8,128)} %get-tuple-element.331, bf16[2,128,1024,1,1]{2,1,0,4,3:T(8,128)(2,1)S(1)} %bitcast.71, pred[]{:T(512)S(6)} %compare.6, bf16[2,2,2,128,128]{4,3,2,1,0:T(8,128)(2,1)S(1)} %bitcast.72, pred[2,2,2]{2,1,0:T(4,128)(4,1)S(1)} %and_bitcast_fusion.3, ...), kind=kOutput, calls=%fused_computation.5.clone.1 | convolution fusion | flops 269746176 | bytes 4980753 | tf_op jit(solution)/shard_map/while/body/eval_jaxpr/ricab,cbh->riah/dot_general | solution.py:45
  75.6 5.2 %collective-permute-done = bf16[256,1024]{1,0:T(8,128)(2,1)S(1)} collective-permute-done((bf16[256,1024]{1,0:T(8,128)(2,1)S(1)}, bf16[256,1024]{1,0:T(8,128)(2,1)S(1)}, u32[]{:S(2)}, u32[]{:S(2)}) %collective-permute-start) | collective-permute-done | bytes 524320 | tf_op jit(solution)/shard_map/while/body/eval_jaxpr/ppermute | solution.py:10
  81.5 2.0 %gather_fusion = bf16[8,128,128]{2,1,0:T(8,128)(2,1)S(1)} fusion(bf16[2,2,12,128,128]{4,3,2,1,0:T(8,128)(2,1)} %get-tuple-element.347, s32[8]{0:T(128)S(1)} %reshape.98), kind=kCustom, calls=%fused_computation.clone.clone.1 | custom fusion | bytes 524384 | tf_op jit(solution)/shard_map/while/body/eval_jaxpr/jit(take_along_axis)/gather | solution.py:42
  83.5 3.4 %bitcast_add_fusion.3 = f32[2,2,128,1024]{3,2,1,0:T(8,128)} fusion(f32[2,2,128,1024]{3,2,1,0:T(8,128)} %get-tuple-element.331, bf16[2,128,1024,1,1]{2,1,0,4,3:T(8,128)(2,1)S(1)} %bitcast.71, pred[]{:T(512)S(6)} %compare.6, bf16[2,2,2,128,128]{4,3,2,1,0:T(8,128)(2,1)S(1)} %bitcast.72, pred[2,2,2]{2,1,0:T(4,128)(4,1)S(1)} %and_bitcast_fusion.3, ...), kind=kOutput, calls=%fused_computation.5.clone.1 | convolution fusion | flops 269746176 | bytes 4980753 | tf_op jit(solution)/shard_map/while/body/eval_jaxpr/ricab,cbh->riah/dot_general | solution.py:45
  87.0 5.2 %collective-permute-done = bf16[256,1024]{1,0:T(8,128)(2,1)S(1)} collective-permute-done((bf16[256,1024]{1,0:T(8,128)(2,1)S(1)}, bf16[256,1024]{1,0:T(8,128)(2,1)S(1)}, u32[]{:S(2)}, u32[]{:S(2)}) %collective-permute-start) | collective-permute-done | bytes 524320 | tf_op jit(solution)/shard_map/while/body/eval_jaxpr/ppermute | solution.py:10
  94.9 3.4 %bitcast_add_fusion.3 = f32[2,2,128,1024]{3,2,1,0:T(8,128)} fusion(f32[2,2,128,1024]{3,2,1,0:T(8,128)} %get-tuple-element.331, bf16[2,128,1024,1,1]{2,1,0,4,3:T(8,128)(2,1)S(1)} %bitcast.71, pred[]{:T(512)S(6)} %compare.6, bf16[2,2,2,128,128]{4,3,2,1,0:T(8,128)(2,1)S(1)} %bitcast.72, pred[2,2,2]{2,1,0:T(4,128)(4,1)S(1)} %and_bitcast_fusion.3, ...), kind=kOutput, calls=%fused_computation.5.clone.1 | convolution fusion | flops 269746176 | bytes 4980753 | tf_op jit(solution)/shard_map/while/body/eval_jaxpr/ricab,cbh->riah/dot_general | solution.py:45
  98.4 5.2 %collective-permute-done = bf16[256,1024]{1,0:T(8,128)(2,1)S(1)} collective-permute-done((bf16[256,1024]{1,0:T(8,128)(2,1)S(1)}, bf16[256,1024]{1,0:T(8,128)(2,1)S(1)}, u32[]{:S(2)}, u32[]{:S(2)}) %collective-permute-start) | collective-permute-done | bytes 524320 | tf_op jit(solution)/shard_map/while/body/eval_jaxpr/ppermute | solution.py:10
  104.3 2.0 %gather_fusion = bf16[8,128,128]{2,1,0:T(8,128)(2,1)S(1)} fusion(bf16[2,2,12,128,128]{4,3,2,1,0:T(8,128)(2,1)} %get-tuple-element.347, s32[8]{0:T(128)S(1)} %reshape.98), kind=kCustom, calls=%fused_computation.clone.clone.1 | custom fusion | bytes 524384 | tf_op jit(solution)/shard_map/while/body/eval_jaxpr/jit(take_along_axis)/gather | solution.py:42
  106.3 3.4 %bitcast_add_fusion.3 = f32[2,2,128,1024]{3,2,1,0:T(8,128)} fusion(f32[2,2,128,1024]{3,2,1,0:T(8,128)} %get-tuple-element.331, bf16[2,128,1024,1,1]{2,1,0,4,3:T(8,128)(2,1)S(1)} %bitcast.71, pred[]{:T(512)S(6)} %compare.6, bf16[2,2,2,128,128]{4,3,2,1,0:T(8,128)(2,1)S(1)} %bitcast.72, pred[2,2,2]{2,1,0:T(4,128)(4,1)S(1)} %and_bitcast_fusion.3, ...), kind=kOutput, calls=%fused_computation.5.clone.1 | convolution fusion | flops 269746176 | bytes 4980753 | tf_op jit(solution)/shard_map/while/body/eval_jaxpr/ricab,cbh->riah/dot_general | solution.py:45
  109.7 5.2 %collective-permute-done = bf16[256,1024]{1,0:T(8,128)(2,1)S(1)} collective-permute-done((bf16[256,1024]{1,0:T(8,128)(2,1)S(1)}, bf16[256,1024]{1,0:T(8,128)(2,1)S(1)}, u32[]{:S(2)}, u32[]{:S(2)}) %collective-permute-start) | collective-permute-done | bytes 524320 | tf_op jit(solution)/shard_map/while/body/eval_jaxpr/ppermute | solution.py:10
  120.8 50.8 %all-gather.2.cloned.1.call-done = f32[2,2,256,1024]{3,2,1,0:T(8,128)} async-done(((f32[1,2,256,1024]{3,2,1,0:T(8,128)}), f32[2,2,256,1024]{3,2,1,0:T(8,128)}) %all-gather.2.cloned.1.call-update) | async-done | bytes 4194320 | tf_op jit(solution)/shard_map/all_gather | solution.py:63
  171.5 4.1 %reduce_sum.35 = f32[2,256,1024]{2,1,0:T(8,128)} reduce(f32[2,2,256,1024]{3,2,1,0:T(8,128)} %all-gather.2.cloned.1.call-done, f32[]{:T(128)} %constant.110.clone.1), dimensions={0}, to_apply=%region_6.8 | reduce | flops 524288 | bytes 6291460 | tf_op jit(solution)/shard_map/reduce_sum | solution.py:63
  175.6 2.0 %divide_convert_fusion = bf16[2,256,1024]{2,1,0:T(8,128)(2,1)S(1)} fusion(f32[2,256,1024]{2,1,0:T(8,128)} %reduce_sum.35, f32[2,256]{1,0:T(2,128)S(1)} %convert_element_type.15), kind=kLoop, calls=%fused_computation.23 | loop fusion | flops 1048576 | bytes 3147776 | tf_op jit(solution)/shard_map/convert.1
  (98 shorter events, 25.7 us)
Async XLA Ops:
  6.5 112.5 %copy-start = (bf16[1024,1024]{1,0:T(8,128)(2,1)S(1)}, bf16[1024,1024]{1,0:T(8,128)(2,1)}, u32[]{:S(2)}) copy-start(bf16[1024,1024]{1,0:T(8,128)(2,1)} %param.17) | copy-start | bytes 6291460
  6.5 28.6 %copy-start.5 = (s32[2,2]{1,0:T(2,128)S(1)}, s32[2,2]{1,0:T(2,128)}, u32[]{:S(2)}) copy-start(s32[2,2]{1,0:T(2,128)} %param.15) | copy-start | bytes 52
  6.5 28.6 %copy-start.4 = (s32[2,2,12]{2,1,0:T(2,128)S(1)}, s32[2,2,12]{2,1,0:T(2,128)}, u32[]{:S(2)}) copy-start(s32[2,2,12]{2,1,0:T(2,128)} %param.14) | copy-start | bytes 580
  6.5 165.0 %all-gather.2.cloned.1.call-start = ((), (), s32[]{:S(2)}) async-start(), calls=%async_computation | async-start | bytes 6291456 | tf_op jit(solution)/shard_map/all_gather | solution.py:63
  6.5 27.5 %collective-permute-start.1 = (bf16[256,1024]{1,0:T(8,128)(2,1)}, bf16[256,1024]{1,0:T(8,128)(2,1)S(1)}, u32[]{:S(2)}, u32[]{:S(2)}) collective-permute-start(bf16[256,1024]{1,0:T(8,128)(2,1)} %param.12), channel_id=1, source_target_pairs={{16,0},{18,2},{20,4},{22,6},{24,8},{26,10},{28,12},{30,14},{0,16},... | collective-permute-start | bytes 1572872 | tf_op jit(solution)/shard_map/ppermute | solution.py:10
  35.2 11.4 %collective-permute-start = (bf16[256,1024]{1,0:T(8,128)(2,1)S(1)}, bf16[256,1024]{1,0:T(8,128)(2,1)S(1)}, u32[]{:S(2)}, u32[]{:S(2)}) collective-permute-start(bf16[256,1024]{1,0:T(8,128)(2,1)S(1)} %copy.18), channel_id=1, source_target_pairs={{30,0},{0,2},{2,4},{4,6},{6,8},{8,10},{10,12},{12,14},{14,16},{16,... | collective-permute-start | bytes 1572872 | tf_op jit(solution)/shard_map/while/body/eval_jaxpr/ppermute | solution.py:10
  46.6 11.4 %collective-permute-start = (bf16[256,1024]{1,0:T(8,128)(2,1)S(1)}, bf16[256,1024]{1,0:T(8,128)(2,1)S(1)}, u32[]{:S(2)}, u32[]{:S(2)}) collective-permute-start(bf16[256,1024]{1,0:T(8,128)(2,1)S(1)} %copy.18), channel_id=1, source_target_pairs={{30,0},{0,2},{2,4},{4,6},{6,8},{8,10},{10,12},{12,14},{14,16},{16,... | collective-permute-start | bytes 1572872 | tf_op jit(solution)/shard_map/while/body/eval_jaxpr/ppermute | solution.py:10
  58.0 11.4 %collective-permute-start = (bf16[256,1024]{1,0:T(8,128)(2,1)S(1)}, bf16[256,1024]{1,0:T(8,128)(2,1)S(1)}, u32[]{:S(2)}, u32[]{:S(2)}) collective-permute-start(bf16[256,1024]{1,0:T(8,128)(2,1)S(1)} %copy.18), channel_id=1, source_target_pairs={{30,0},{0,2},{2,4},{4,6},{6,8},{8,10},{10,12},{12,14},{14,16},{16,... | collective-permute-start | bytes 1572872 | tf_op jit(solution)/shard_map/while/body/eval_jaxpr/ppermute | solution.py:10
  69.4 11.4 %collective-permute-start = (bf16[256,1024]{1,0:T(8,128)(2,1)S(1)}, bf16[256,1024]{1,0:T(8,128)(2,1)S(1)}, u32[]{:S(2)}, u32[]{:S(2)}) collective-permute-start(bf16[256,1024]{1,0:T(8,128)(2,1)S(1)} %copy.18), channel_id=1, source_target_pairs={{30,0},{0,2},{2,4},{4,6},{6,8},{8,10},{10,12},{12,14},{14,16},{16,... | collective-permute-start | bytes 1572872 | tf_op jit(solution)/shard_map/while/body/eval_jaxpr/ppermute | solution.py:10
  80.8 11.4 %collective-permute-start = (bf16[256,1024]{1,0:T(8,128)(2,1)S(1)}, bf16[256,1024]{1,0:T(8,128)(2,1)S(1)}, u32[]{:S(2)}, u32[]{:S(2)}) collective-permute-start(bf16[256,1024]{1,0:T(8,128)(2,1)S(1)} %copy.18), channel_id=1, source_target_pairs={{30,0},{0,2},{2,4},{4,6},{6,8},{8,10},{10,12},{12,14},{14,16},{16,... | collective-permute-start | bytes 1572872 | tf_op jit(solution)/shard_map/while/body/eval_jaxpr/ppermute | solution.py:10
  92.2 11.4 %collective-permute-start = (bf16[256,1024]{1,0:T(8,128)(2,1)S(1)}, bf16[256,1024]{1,0:T(8,128)(2,1)S(1)}, u32[]{:S(2)}, u32[]{:S(2)}) collective-permute-start(bf16[256,1024]{1,0:T(8,128)(2,1)S(1)} %copy.18), channel_id=1, source_target_pairs={{30,0},{0,2},{2,4},{4,6},{6,8},{8,10},{10,12},{12,14},{14,16},{16,... | collective-permute-start | bytes 1572872 | tf_op jit(solution)/shard_map/while/body/eval_jaxpr/ppermute | solution.py:10
  103.6 11.4 %collective-permute-start = (bf16[256,1024]{1,0:T(8,128)(2,1)S(1)}, bf16[256,1024]{1,0:T(8,128)(2,1)S(1)}, u32[]{:S(2)}, u32[]{:S(2)}) collective-permute-start(bf16[256,1024]{1,0:T(8,128)(2,1)S(1)} %copy.18), channel_id=1, source_target_pairs={{30,0},{0,2},{2,4},{4,6},{6,8},{8,10},{10,12},{12,14},{14,16},{16,... | collective-permute-start | bytes 1572872 | tf_op jit(solution)/shard_map/while/body/eval_jaxpr/ppermute | solution.py:10
  114.9 1.7 copy-start.1
  118.3 0.7 copy-start.6
  175.6 2.2 %copy-start.2 = (bf16[1024,1024]{1,0:T(8,128)(2,1)S(1)}, bf16[1024,1024]{1,0:T(8,128)(2,1)}, u32[]{:S(2)}) copy-start(bf16[1024,1024]{1,0:T(8,128)(2,1)} %param.18) | copy-start | bytes 6291460
  177.8 1.6 copy-start.3
Sparse Core Ops, SparseCore 0:
  118.5 52.9 all-gather.1
